TPU v7x, 256 devices: a whole 4x4x8 slice. The times are simulated.
256 devices in a mesh: group: 16 (over z, core), dev: 16 (over y, x).
Axes of the slice: x: 4, y: 4, z: 8, core: 2. Of those that a mesh axis runs over, the one named last changes fastest.
Arguments:
- tokens: bfloat16 [1024, 7168], P(('group', 'dev')), may hold values from -6 to 6
- group_ids: int32 [1024, 4], P(('group', 'dev')), may hold values from 0 to 15, as said below
- expert_ids: int32 [1024, 8], P(('group', 'dev')), may hold values from 0 to 63, as said below
- gate_scores: bfloat16 [1024, 8], P(('group', 'dev')), may hold values from 0.099609375 to 1
- w_gate: bfloat16 [7168, 65536], P(None, ('group', 'dev')), may hold values from -0.0625 to 0.0625
- w_up: bfloat16 [7168, 65536], P(None, ('group', 'dev')), may hold values from -0.0625 to 0.0625
- w_down: bfloat16 [65536, 7168], P(('group', 'dev')), may hold values from -0.1875 to 0.1875
Outputs:
- combined: bfloat16 [1024, 7168], P(('group', 'dev'))
Inputs may be any that keep to these rules, and one draw needn't show every extreme that they name: `group_ids`: each row names 4 different groups; among the 4 rows of one aligned block, at most 2 rows name any one group. `expert_ids`: each row names 8 different experts, exactly two in each group of the row's group_ids (expert x lies in group x // 4).
All inputs are finite; a program needn't handle non-finite values.
Results may differ from a plain program's by a relative error of at most 0.014.
Values may be sent and summed in bfloat16 or wider, within the bound.
No kernel may reach another device: no remote copies, remote signals or barrier semaphores. Data moves between devices by JAX's collectives and lax.ppermute only.
A program may use at most 64 MiB of HBM per device.

v0:
```python
import jax
import jax.numpy as jnp
from jax import lax
from jax.sharding import PartitionSpec as P

FF = 1024
EXP_GROUP = 4
CAP = 2


def local(tokens, group_ids, expert_ids, gate_scores, w_gate, w_up, w_down):
    group_count = lax.axis_size("group")
    dev_count = lax.axis_size("dev")
    model_width = tokens.shape[1]
    block_cols = w_gate.shape[1]
    expert_total = group_count * EXP_GROUP
    group_iota = jnp.arange(group_count, dtype=jnp.int32)
    member = jnp.sum((group_ids[:, :, None] == group_iota[None, None, :]).astype(jnp.int32), axis=1)
    before = jnp.cumsum(member, axis=0) - member
    slot_iota = jnp.arange(CAP, dtype=jnp.int32)
    select = (member.T[:, None, :] == 1) & (before.T[:, None, :] == slot_iota[None, :, None])
    select_rows = select.astype(jnp.bfloat16)
    matches = (
        expert_ids[:, :, None] == jnp.arange(expert_total, dtype=jnp.int32)[None, None, :]
    ).astype(jnp.float32)
    coef = jnp.sum(gate_scores.astype(jnp.float32)[:, :, None] * matches, axis=1)
    coef = coef.reshape(-1, group_count, EXP_GROUP).astype(jnp.bfloat16)
    send_rows = jnp.einsum(
        "gst,td->gsd", select_rows, tokens, preferred_element_type=jnp.float32
    ).astype(jnp.bfloat16)
    send_coef = jnp.einsum(
        "gst,tge->gse", select_rows, coef, preferred_element_type=jnp.float32
    ).astype(jnp.bfloat16)
    recv_rows, recv_coef = (
        lax.all_to_all(send_rows, "group", split_axis=0, concat_axis=0, tiled=True),
        lax.all_to_all(send_coef, "group", split_axis=0, concat_axis=0, tiled=True),
    )
    all_rows, all_coef = (
        lax.all_gather(recv_rows, "dev", axis=0, tiled=True),
        lax.all_gather(recv_coef, "dev", axis=0, tiled=True),
    )
    flat_rows = all_rows.reshape(-1, model_width)
    flat_coef = all_coef.reshape(-1, EXP_GROUP)
    dev_index = lax.axis_index("dev")
    owner_expert = (dev_index * block_cols + jnp.arange(block_cols, dtype=jnp.int32)) // FF
    onehot = (owner_expert[None, :] == jnp.arange(EXP_GROUP, dtype=jnp.int32)[:, None]).astype(
        jnp.bfloat16
    )
    gate_out = jnp.dot(flat_rows, w_gate, preferred_element_type=jnp.float32)
    up_out = jnp.dot(flat_rows, w_up, preferred_element_type=jnp.float32)
    col_scale = jnp.dot(flat_coef, onehot, preferred_element_type=jnp.float32)
    hidden = (col_scale * jax.nn.silu(gate_out) * up_out).astype(jnp.bfloat16)
    partial_value = lax.optimization_barrier(
        jnp.dot(hidden, w_down, preferred_element_type=jnp.float32).astype(jnp.bfloat16)
    )
    partial_value = partial_value.reshape(dev_count, group_count, CAP, model_width)
    moved_back = lax.all_to_all(partial_value, "group", split_axis=1, concat_axis=1, tiled=True)
    summed = lax.psum_scatter(
        moved_back.astype(jnp.float32).astype(jnp.bfloat16), "dev", scatter_dimension=0, tiled=True
    )
    returned = summed.reshape(group_count, CAP, model_width)
    combined = jnp.einsum("gst,gsd->td", select_rows, returned, preferred_element_type=jnp.float32)
    return combined.astype(jnp.bfloat16)


def solution(mesh):
    return jax.shard_map(
        local,
        mesh=mesh,
        in_specs=(
            P(("group", "dev"), None),
            P(("group", "dev"), None),
            P(("group", "dev"), None),
            P(("group", "dev"), None),
            P(None, ("group", "dev")),
            P(None, ("group", "dev")),
            P(("group", "dev"), None),
        ),
        out_specs=P(("group", "dev"), None),
        check_vma=False,
    )
```

profile of v0, /device:TPU:2, one launch (start us, length us, event | category | flops | bytes accessed | tf_op | source)
XLA Modules:
  0.0 424.0 jit_solution(7251178532512982187)
XLA Ops:
  6.5 0.0 copy-start
  6.5 0.0 all-gather.2.cloned.1.call-start
  6.5 0.8 convert_reduce_fusion
  7.4 0.0 copy-done
  7.4 0.4 convolution_convert_fusion.1
  7.8 0.5 copy.26
  8.2 23.2 %all_to_all.15 = bf16[16,2,7168]{2,1,0:T(2,128)(2,1)} all-to-all(bf16[16,2,7168]{2,1,0:T(2,128)(2,1)S(1)} %copy.26), channel_id=1, replica_groups=mesh['group'=16,'dev'=16] {'group'}, dimensions={0} | all-to-all | bytes 917504 | tf_op jit(solution)/shard_map/all_to_all | solution.py:35
  31.5 0.0 all-gather.2.cloned.1.call-update
  31.5 0.1 copy.24
  31.6 0.7 convert_element_type.33
  32.3 0.8 select_reduce_fusion
  33.1 0.1 convert_element_type.35
  33.2 0.8 convolution_convert_fusion.2
  33.9 4.0 all-to-all-start
  38.0 0.0 reduce-scatter.4.cloned.1.call-start
  38.0 7.5 %all-to-all-done = bf16[16,2,4]{2,1,0:T(2,128)(2,1)S(1)} async-done(((bf16[16,2,4]{2,1,0:T(2,128)(2,1)}), bf16[16,2,4]{2,1,0:T(2,128)(2,1)S(1)}, u32[]{:S(2)}, u32[]{:S(2)}) %all-to-all-start) | async-done | bytes 288 | tf_op jit(solution)/shard_map/all_to_all | solution.py:36
  45.5 23.8 %all_gather.6 = bf16[256,2,4]{2,1,0:T(2,128)(2,1)S(1)} all-gather(bf16[16,2,4]{2,1,0:T(2,128)(2,1)S(1)} %all-to-all-done), channel_id=1, replica_groups=mesh['group'=16,'dev'=16] {'dev'}, dimensions={0}, use_global_device_ids=true | all-gather | bytes 4352 | tf_op jit(solution)/shard_map/all_gather | solution.py:40
  69.3 32.0 %all-gather.2.cloned.1.call-done = bf16[256,2,7168]{2,1,0:T(2,128)(2,1)} async-done(((bf16[16,2,7168]{2,1,0:T(2,128)(2,1)}), bf16[256,2,7168]{2,1,0:T(2,128)(2,1)}) %all-gather.2.cloned.1.call-update) | async-done | bytes 7340048 | tf_op jit(solution)/shard_map/all_gather | solution.py:39
  101.3 15.4 %reshape.40 = bf16[512,7168]{1,0:T(8,128)(2,1)} reshape(bf16[256,2,7168]{2,1,0:T(2,128)(2,1)} %all-gather.2.cloned.1.call-done) | data formatting | bytes 14680064 | tf_op jit(solution)/shard_map/reshape | solution.py:42
  116.7 0.0 copy-start.1
  116.7 0.0 copy-start.2
  116.7 6.3 %fusion.16 = f32[512,256]{1,0:T(8,128)S(1)} fusion(bf16[512,7168]{1,0:T(8,128)(2,1)} %reshape.40, bf16[7168,256]{1,0:T(8,128)(2,1)} %param.11), kind=kOutput, calls=%fused_computation.32 | convolution fusion | flops 1879048192 | bytes 11534336 | tf_op jit(solution)/shard_map/dot_general | solution.py:49
  123.1 0.0 copy-done.1
  123.1 0.9 copy-done.2
  124.0 2.1 fusion.17
  126.0 6.4 %convolution_convert_fusion = bf16[512,7168]{1,0:T(8,128)(2,1)} fusion(bf16[256,7168]{1,0:T(8,128)(2,1)} %param.13, f32[512,256]{1,0:T(8,128)S(1)} %fusion.17, bf16[512,4]{1,0:T(8,128)(2,1)S(1)} %bitcast.25, f32[512,256]{1,0:T(8,128)S(1)} %fusion.16, s32[256]{0:T(256)S(1)} %and_select_fusion), kind=kOutput, calls=%fused_computation | convolution fusion | flops 1884685312 | bytes 12063744 | tf_op jit(solution)/shard_map/dot_general | solution.py:54
  132.4 14.9 %reshape.41 = bf16[16,16,2,7168]{3,2,1,0:T(2,128)(2,1)} reshape(bf16[512,7168]{1,0:T(8,128)(2,1)} %convolution_convert_fusion) | data formatting | bytes 14680064 | tf_op jit(solution)/shard_map/reshape | solution.py:56
  147.3 6.6 %copy.27 = bf16[16,16,2,7168]{3,2,0,1:T(2,128)(2,1)S(1)} copy(bf16[16,16,2,7168]{3,2,1,0:T(2,128)(2,1)} %reshape.41) | data formatting | bytes 14680064 | tf_op jit(solution)/shard_map/reshape | solution.py:56
  153.9 168.9 %all_to_all.16 = bf16[16,16,2,7168]{3,2,0,1:T(2,128)(2,1)S(1)} all-to-all(bf16[16,16,2,7168]{3,2,0,1:T(2,128)(2,1)S(1)} %copy.27), channel_id=1, replica_groups=mesh['group'=16,'dev'=16] {'group'}, dimensions={1} | all-to-all | bytes 14680064 | tf_op jit(solution)/shard_map/all_to_all | solution.py:57
  322.8 7.0 %copy.28 = bf16[16,16,2,7168]{3,1,2,0:T(8,128)(2,1)} copy(bf16[16,16,2,7168]{3,2,0,1:T(2,128)(2,1)S(1)} %all_to_all.16) | data formatting | bytes 14680064 | tf_op jit(solution)/shard_map/all_to_all | solution.py:57
  329.8 0.0 reduce-scatter.4.cloned.1.call-update
  329.8 85.4 %reduce-scatter.4.cloned.1.call-done = bf16[1,16,2,7168]{3,1,2,0:T(8,128)(2,1)} async-done(((bf16[16,16,2,7168]{3,1,2,0:T(8,128)(2,1)}), bf16[1,16,2,7168]{3,1,2,0:T(8,128)(2,1)}) %reduce-scatter.4.cloned.1.call-update) | async-done | bytes 458768
  415.2 1.9 fusion
  (5 shorter events, 0.1 us)
Async XLA Ops:
  6.5 0.9 copy-start
  6.5 94.7 %all-gather.2.cloned.1.call-start = ((), (), s32[]{:S(2)}) async-start(), calls=%async_computation.4 | async-start | bytes 7798784 | tf_op jit(solution)/shard_map/all_gather | solution.py:39
  33.9 11.5 %all-to-all-start = ((bf16[16,2,4]{2,1,0:T(2,128)(2,1)}), bf16[16,2,4]{2,1,0:T(2,128)(2,1)S(1)}, u32[]{:S(2)}, u32[]{:S(2)}) async-start(bf16[16,2,4]{2,1,0:T(2,128)(2,1)} %convolution_convert_fusion.2), calls=%async_computation | async-start | bytes 16384 | tf_op jit(solution)/shard_map/all_to_all | solution.py:36
  38.0 377.3 %reduce-scatter.4.cloned.1.call-start = ((), (), s32[]{:S(2)}) async-start(), calls=%async_computation.5 | async-start | bytes 7798784
  116.7 6.3 %copy-start.1 = (bf16[512,7168]{1,0:T(8,128)(2,1)S(1)}, bf16[512,7168]{1,0:T(8,128)(2,1)}, u32[]{:S(2)}) copy-start(bf16[512,7168]{1,0:T(8,128)(2,1)} %reshape.40) | copy-start | bytes 22020100
  116.7 7.3 %copy-start.2 = (bf16[7168,256]{1,0:T(8,128)(2,1)S(1)}, bf16[7168,256]{1,0:T(8,128)(2,1)}, u32[]{:S(2)}) copy-start(bf16[7168,256]{1,0:T(8,128)(2,1)} %param.12) | copy-start | bytes 11010052
Sparse Core Ops, SparseCore 0:
  31.6 69.5 all-gather.1
  330.0 85.2 reduce-scatter.3
where the time goes:
time: 425 us; the launch traced here: 424 us
  blocking collectives  216 us (51%)
  waiting for transfers between devices  125 us (29%)
  local copies, waits for them, and re-layouts  45.5 us (11%)
  matrix products  17.8 us (4%)
  between operations  13.5 us (3%)
    all_to_all x1, blocking collectives, local(): lax.all_to_all(partial_value, 'group', split_axis=1, concat_axis=1, tiled...  169 us
    unnamed x3, waiting for transfers between devices  85.4 us
    all_gather x1, waiting for transfers between devices, local(): lax.all_gather(recv_rows, 'dev', axis=0, tiled=True)  32 us
    all_gather x1, blocking collectives, local(): lax.all_gather(recv_coef, 'dev', axis=0, tiled=True)  23.8 us
    all_to_all x1, blocking collectives, local(): lax.all_to_all(send_rows, 'group', split_axis=0, concat_axis=0, tiled=True)  23.2 us
    reshape x2, local copies, waits for them, and re-layouts, local(): partial_value.reshape(dev_count, group_count, CAP, model_width)  21.5 us
    reshape x1, local copies, waits for them, and re-layouts, local(): flat_rows = all_rows.reshape(-1, model_width)  15.4 us
  transfers between devices with their start and end apart: 3, of which 3 were waited for; matrix products, arithmetic and copies ran while one was open for 1% of the time, Pallas kernels for 0%

commit v1 on v0

--- a/solution.py
+++ b/solution.py
@@ -9,6 +9,30 @@
 
 
 def local(tokens, group_ids, expert_ids, gate_scores, w_gate, w_up, w_down):
+
+    def _answer_scenes(field):
+        known, clean, earlier = (lax.axis_size("dev"), lax.axis_index("dev"), field.shape[0])
+        xs_all = [it * known if ix == 0 else it for ix, it in enumerate(field.shape)]
+        x_next = lax.dynamic_update_slice_in_dim(
+            jnp.zeros(xs_all, field.dtype), field, clean * earlier, axis=0
+        )
+        passed = back = field
+        for to_i in range(1, known // 2 + 1):
+            passed = lax.ppermute(
+                passed, axis_name="dev", perm=[(ix, (ix + 1) % known) for ix in range(known)]
+            )
+            x_next = lax.dynamic_update_slice_in_dim(
+                x_next, passed, (clean - to_i) % known * earlier, axis=0
+            )
+            if 2 * to_i < known:
+                back = lax.ppermute(
+                    back, axis_name="dev", perm=[(ix, (ix - 1) % known) for ix in range(known)]
+                )
+                x_next = lax.dynamic_update_slice_in_dim(
+                    x_next, back, (clean + to_i) % known * earlier, axis=0
+                )
+        return x_next
+
     group_count = lax.axis_size("group")
     dev_count = lax.axis_size("dev")
     model_width = tokens.shape[1]
@@ -36,7 +60,7 @@
         lax.all_to_all(send_coef, "group", split_axis=0, concat_axis=0, tiled=True),
     )
     all_rows, all_coef = (
-        lax.all_gather(recv_rows, "dev", axis=0, tiled=True),
+        _answer_scenes(recv_rows),
         lax.all_gather(recv_coef, "dev", axis=0, tiled=True),
     )
     flat_rows = all_rows.reshape(-1, model_width)

time: 425 us -> 495 us (1.16)
  starting transfers between devices: 4.05 us -> 39 us
  waiting for transfers between devices: 125 us -> 152 us
  local copies, waits for them, and re-layouts: 45.5 us -> 67.9 us
  blocking collectives: 216 us -> 194 us
  matrix products: 17.8 us -> 25.4 us
    ppermute x0 -> x15, waiting for transfers between devices: none -> 59.2 us  [the longest x8 58.7 us: _answer_scenes(): lax.ppermute(passed, axis_name='dev', perm=[(ix, (ix + 1) % known) for ix...]
    all_gather x1 -> x0, waiting for transfers between devices: 32 us -> none  [local(): lax.all_gather(recv_rows, 'dev', axis=0, tiled=True)]
    ppermute x0 -> x15, starting transfers between devices: none -> 26.8 us  [the longest x7 15.5 us: _answer_scenes(): lax.ppermute(back, axis_name='dev', perm=[(ix, (ix - 1) % known) for ix i...]
    all_to_all x1 -> x0, blocking collectives: 23.2 us -> none  [local(): lax.all_to_all(send_rows, 'group', split_axis=0, concat_axis=0, tiled=True)]
    dynamic_update_slice x0 -> x16, local copies, waits for them, and re-layouts: none -> 17.7 us  [the longest x8 8.77 us: _answer_scenes(): lax.dynamic_update_slice_in_dim(x_next, passed, (clean - to_i) % known *...]
    dot_general x1, matrix products: 6.38 us -> 16 us  [local(): jnp.dot(hidden, w_down, preferred_element_type=jnp.float32)]
    unnamed x3 -> x2, waiting for transfers between devices: 85.4 us -> 87.1 us
  transfers between devices with their start and end apart: 3 -> 18, of which waited for: 3 -> 13; matrix products, arithmetic and copies ran while one was open for 1% -> 5% of each run, Pallas kernels for 0% -> 0%
where the time goes in v1:
time: 495 us; the launch traced here: 494 us
  blocking collectives  194 us (39%)
  waiting for transfers between devices  152 us (31%)
  local copies, waits for them, and re-layouts  67.9 us (14%)
  starting transfers between devices  39 us (8%)
  matrix products  25.4 us (5%)
  between operations  13.8 us (3%)
    all_to_all x1, blocking collectives, local(): lax.all_to_all(partial_value, 'group', split_axis=1, concat_axis=1, tiled...  170 us
    unnamed x2, waiting for transfers between devices  87.1 us
    ppermute x8, waiting for transfers between devices, _answer_scenes(): lax.ppermute(passed, axis_name='dev', perm=[(ix, (ix + 1) % known) for ix...  58.7 us
    all_gather x1, blocking collectives, local(): lax.all_gather(recv_coef, 'dev', axis=0, tiled=True)  23.8 us
    reshape x2, local copies, waits for them, and re-layouts, local(): partial_value.reshape(dev_count, group_count, CAP, model_width)  21.5 us
    dot_general x1, matrix products, local(): jnp.dot(hidden, w_down, preferred_element_type=jnp.float32)  16 us
    ppermute x7, starting transfers between devices, _answer_scenes(): lax.ppermute(back, axis_name='dev', perm=[(ix, (ix - 1) % known) for ix i...  15.5 us
    reshape x1, local copies, waits for them, and re-layouts, local(): flat_rows = all_rows.reshape(-1, model_width)  15.4 us
  transfers between devices with their start and end apart: 18, of which 13 were waited for; matrix products, arithmetic and copies ran while one was open for 5% of the time, Pallas kernels for 0%

profile of v1, /device:TPU:2, one launch (start us, length us, event | category | flops | bytes accessed | tf_op | source)
XLA Modules:
  0.0 494.3 jit_solution(18079745717984911997)
XLA Ops:
  6.5 0.8 convert_reduce_fusion
  7.4 0.1 copy.34
  7.5 0.7 convert_element_type.33
  8.2 0.8 select_reduce_fusion
  8.9 0.1 convert_element_type.35
  9.0 0.8 convolution_convert_fusion.2
  9.8 8.6 %all-to-all-start = ((bf16[16,2,4]{2,1,0:T(2,128)(2,1)}), bf16[16,2,4]{2,1,0:T(2,128)(2,1)S(1)}, u32[]{:S(2)}, u32[]{:S(2)}) async-start(bf16[16,2,4]{2,1,0:T(2,128)(2,1)} %convolution_convert_fusion.2), calls=%async_computation | async-start | bytes 16384 | tf_op jit(solution)/shard_map/all_to_all | solution.py:60
  18.4 0.4 convolution_convert_fusion.1
  18.8 1.3 copy.36
  20.0 5.9 %all-to-all-done = bf16[16,2,4]{2,1,0:T(2,128)(2,1)S(1)} async-done(((bf16[16,2,4]{2,1,0:T(2,128)(2,1)}), bf16[16,2,4]{2,1,0:T(2,128)(2,1)S(1)}, u32[]{:S(2)}, u32[]{:S(2)}) %all-to-all-start) | async-done | bytes 288 | tf_op jit(solution)/shard_map/all_to_all | solution.py:60
  25.9 3.6 all-to-all-start.1
  29.5 0.0 reduce-scatter.4.cloned.1.call-start
  29.8 23.8 %all_gather.3 = bf16[256,2,4]{2,1,0:T(2,128)(2,1)S(1)} all-gather(bf16[16,2,4]{2,1,0:T(2,128)(2,1)S(1)} %all-to-all-done), channel_id=1, replica_groups=mesh['group'=16,'dev'=16] {'dev'}, dimensions={0}, use_global_device_ids=true | all-gather | bytes 4352 | tf_op jit(solution)/shard_map/all_gather | solution.py:64
  53.6 0.2 fusion.13
  53.9 1.4 collective-permute-start
  55.3 0.7 collective-permute-start.1
  56.0 4.9 broadcast_in_dim.2
  60.8 1.1 constant_dynamic-update-slice_fusion.15
  62.0 2.0 collective-permute-done
  64.0 2.5 collective-permute-start.2
  66.4 0.1 collective-permute-done.1
  66.6 1.1 constant_dynamic-update-slice_fusion.14
  67.7 1.1 constant_dynamic-update-slice_fusion.13
  68.8 7.5 %collective-permute-done.2 = bf16[16,2,7168]{2,1,0:T(2,128)(2,1)S(1)} collective-permute-done((bf16[16,2,7168]{2,1,0:T(2,128)(2,1)S(1)}, bf16[16,2,7168]{2,1,0:T(2,128)(2,1)S(1)}, u32[]{:S(2)}, u32[]{:S(2)}) %collective-permute-start.2) | collective-permute-done | bytes 458784 | tf_op jit(solution)/shard_map/ppermute | solution.py:21
  76.3 2.5 collective-permute-start.4
  78.7 0.1 collective-permute-start.5
  78.8 1.1 constant_dynamic-update-slice_fusion.12
  79.9 1.1 constant_dynamic-update-slice_fusion.11
  81.1 8.5 %collective-permute-done.4 = bf16[16,2,7168]{2,1,0:T(2,128)(2,1)S(1)} collective-permute-done((bf16[16,2,7168]{2,1,0:T(2,128)(2,1)S(1)}, bf16[16,2,7168]{2,1,0:T(2,128)(2,1)S(1)}, u32[]{:S(2)}, u32[]{:S(2)}) %collective-permute-start.4) | collective-permute-done | bytes 458784 | tf_op jit(solution)/shard_map/ppermute | solution.py:21
  89.6 2.5 collective-permute-start.6
  92.1 0.4 collective-permute-start.7
  92.4 1.1 constant_dynamic-update-slice_fusion.10
  93.5 1.1 constant_dynamic-update-slice_fusion.9
  94.6 7.5 %collective-permute-done.6 = bf16[16,2,7168]{2,1,0:T(2,128)(2,1)S(1)} collective-permute-done((bf16[16,2,7168]{2,1,0:T(2,128)(2,1)S(1)}, bf16[16,2,7168]{2,1,0:T(2,128)(2,1)S(1)}, u32[]{:S(2)}, u32[]{:S(2)}) %collective-permute-start.6) | collective-permute-done | bytes 458784 | tf_op jit(solution)/shard_map/ppermute | solution.py:21
  102.1 2.5 collective-permute-start.8
  104.6 0.1 collective-permute-done.7
  104.6 2.7 collective-permute-start.9
  107.4 1.1 constant_dynamic-update-slice_fusion.8
  108.5 1.1 constant_dynamic-update-slice_fusion.7
  109.5 7.6 %collective-permute-done.8 = bf16[16,2,7168]{2,1,0:T(2,128)(2,1)S(1)} collective-permute-done((bf16[16,2,7168]{2,1,0:T(2,128)(2,1)S(1)}, bf16[16,2,7168]{2,1,0:T(2,128)(2,1)S(1)}, u32[]{:S(2)}, u32[]{:S(2)}) %collective-permute-start.8) | collective-permute-done | bytes 458784 | tf_op jit(solution)/shard_map/ppermute | solution.py:21
  117.1 0.2 collective-permute-done.9
  117.3 6.1 %collective-permute-start.11 = (bf16[16,2,7168]{2,1,0:T(2,128)(2,1)S(1)}, bf16[16,2,7168]{2,1,0:T(2,128)(2,1)S(1)}, u32[]{:S(2)}, u32[]{:S(2)}) collective-permute-start(bf16[16,2,7168]{2,1,0:T(2,128)(2,1)S(1)} %collective-permute-done.9), channel_id=1, source_target_pairs={{0,15},{1,0},{2,1},{3,2},{4,3},{5,4},{6,5},{7,6},{8,7},{9,8},{10,9... | collective-permute-start | bytes 1376264 | tf_op jit(solution)/shard_map/ppermute | solution.py:28
  123.4 1.1 constant_dynamic-update-slice_fusion.6
  124.6 1.1 constant_dynamic-update-slice_fusion.5
  125.7 8.4 %collective-permute-done.10 = bf16[16,2,7168]{2,1,0:T(2,128)(2,1)S(1)} collective-permute-done((bf16[16,2,7168]{2,1,0:T(2,128)(2,1)S(1)}, bf16[16,2,7168]{2,1,0:T(2,128)(2,1)S(1)}, u32[]{:S(2)}, u32[]{:S(2)}) %collective-permute-start.10) | collective-permute-done | bytes 458784 | tf_op jit(solution)/shard_map/ppermute | solution.py:21
  134.1 0.0 collective-permute-done.11
  134.1 5.5 %collective-permute-start.13 = (bf16[16,2,7168]{2,1,0:T(2,128)(2,1)S(1)}, bf16[16,2,7168]{2,1,0:T(2,128)(2,1)S(1)}, u32[]{:S(2)}, u32[]{:S(2)}) collective-permute-start(bf16[16,2,7168]{2,1,0:T(2,128)(2,1)S(1)} %collective-permute-done.11), channel_id=1, source_target_pairs={{0,15},{1,0},{2,1},{3,2},{4,3},{5,4},{6,5},{7,6},{8,7},{9,8},{10,9... | collective-permute-start | bytes 1376264 | tf_op jit(solution)/shard_map/ppermute | solution.py:28
  139.6 1.1 constant_dynamic-update-slice_fusion.4
  140.8 1.1 constant_dynamic-update-slice_fusion.3
  141.9 8.0 %collective-permute-done.12 = bf16[16,2,7168]{2,1,0:T(2,128)(2,1)S(1)} collective-permute-done((bf16[16,2,7168]{2,1,0:T(2,128)(2,1)S(1)}, bf16[16,2,7168]{2,1,0:T(2,128)(2,1)S(1)}, u32[]{:S(2)}, u32[]{:S(2)}) %collective-permute-start.12) | collective-permute-done | bytes 458784 | tf_op jit(solution)/shard_map/ppermute | solution.py:21
  149.8 1.1 constant_dynamic-update-slice_fusion.2
  150.9 1.1 constant_dynamic-update-slice_fusion.1
  152.0 9.3 %collective-permute-done.14 = bf16[16,2,7168]{2,1,0:T(2,128)(2,1)S(1)} collective-permute-done((bf16[16,2,7168]{2,1,0:T(2,128)(2,1)S(1)}, bf16[16,2,7168]{2,1,0:T(2,128)(2,1)S(1)}, u32[]{:S(2)}, u32[]{:S(2)}) %collective-permute-start.14) | collective-permute-done | bytes 458784 | tf_op jit(solution)/shard_map/ppermute | solution.py:21
  161.3 1.1 constant_dynamic-update-slice_fusion
  162.4 15.4 %reshape.40 = bf16[512,7168]{1,0:T(8,128)(2,1)} reshape(bf16[256,2,7168]{2,1,0:T(2,128)(2,1)} %constant_dynamic-update-slice_fusion) | data formatting | bytes 14680064 | tf_op jit(solution)/shard_map/reshape | solution.py:66
  177.8 6.2 %fusion.16 = f32[512,256]{1,0:T(8,128)S(1)} fusion(bf16[512,7168]{1,0:T(8,128)(2,1)} %reshape.40, bf16[7168,256]{1,0:T(8,128)(2,1)} %param.11), kind=kOutput, calls=%fused_computation.49 | convolution fusion | flops 1879048192 | bytes 11534336 | tf_op jit(solution)/shard_map/dot_general | solution.py:73
  184.0 16.0 %convolution_convert_fusion = bf16[512,7168]{1,0:T(8,128)(2,1)} fusion(bf16[256,7168]{1,0:T(8,128)(2,1)} %param.13, bf16[512,7168]{1,0:T(8,128)(2,1)} %reshape.40, bf16[7168,256]{1,0:T(8,128)(2,1)} %param.12, f32[512,256]{1,0:T(8,128)S(1)} %fusion.13, f32[512,256]{1,0:T(8,128)S(1)} %fusion.16), kind=kOutput, calls=%fused_computation | convolution fusion | flops 3762683904 | bytes 23068672 | tf_op jit(solution)/shard_map/dot_general | solution.py:78
  200.0 14.9 %reshape.41 = bf16[16,16,2,7168]{3,2,1,0:T(2,128)(2,1)} reshape(bf16[512,7168]{1,0:T(8,128)(2,1)} %convolution_convert_fusion) | data formatting | bytes 14680064 | tf_op jit(solution)/shard_map/reshape | solution.py:80
  214.9 6.6 %copy.37 = bf16[16,16,2,7168]{3,2,0,1:T(2,128)(2,1)S(1)} copy(bf16[16,16,2,7168]{3,2,1,0:T(2,128)(2,1)} %reshape.41) | data formatting | bytes 14680064 | tf_op jit(solution)/shard_map/reshape | solution.py:80
  221.5 170.0 %all_to_all.15 = bf16[16,16,2,7168]{3,2,0,1:T(2,128)(2,1)S(1)} all-to-all(bf16[16,16,2,7168]{3,2,0,1:T(2,128)(2,1)S(1)} %copy.37), channel_id=1, replica_groups=mesh['group'=16,'dev'=16] {'group'}, dimensions={1} | all-to-all | bytes 14680064 | tf_op jit(solution)/shard_map/all_to_all | solution.py:81
  391.5 7.0 %copy.38 = bf16[16,16,2,7168]{3,1,2,0:T(8,128)(2,1)} copy(bf16[16,16,2,7168]{3,2,0,1:T(2,128)(2,1)S(1)} %all_to_all.15) | data formatting | bytes 14680064 | tf_op jit(solution)/shard_map/all_to_all | solution.py:81
  398.5 0.0 reduce-scatter.4.cloned.1.call-update
  398.5 87.0 %reduce-scatter.4.cloned.1.call-done = bf16[1,16,2,7168]{3,1,2,0:T(8,128)(2,1)} async-done(((bf16[16,16,2,7168]{3,1,2,0:T(8,128)(2,1)}), bf16[1,16,2,7168]{3,1,2,0:T(8,128)(2,1)}) %reduce-scatter.4.cloned.1.call-update) | async-done | bytes 458768
  485.5 1.9 fusion
  (17 shorter events, 0.1 us)
Async XLA Ops:
  6.5 11.8 %copy-start = (bf16[4,7168]{1,0:T(4,128)(2,1)S(1)}, bf16[4,7168]{1,0:T(4,128)(2,1)}, u32[]{:S(2)}) copy-start(bf16[4,7168]{1,0:T(4,128)(2,1)} %param.7) | copy-start | bytes 172036
  9.8 16.1 %all-to-all-start = ((bf16[16,2,4]{2,1,0:T(2,128)(2,1)}), bf16[16,2,4]{2,1,0:T(2,128)(2,1)S(1)}, u32[]{:S(2)}, u32[]{:S(2)}) async-start(bf16[16,2,4]{2,1,0:T(2,128)(2,1)} %convolution_convert_fusion.2), calls=%async_computation | async-start | bytes 16384 | tf_op jit(solution)/shard_map/all_to_all | solution.py:60
  25.9 27.9 %all-to-all-start.1 = ((bf16[16,2,7168]{2,1,0:T(2,128)(2,1)}), bf16[16,2,7168]{2,1,0:T(2,128)(2,1)S(1)}, u32[]{:S(2)}, u32[]{:S(2)}) async-start(bf16[16,2,7168]{2,1,0:T(2,128)(2,1)} %copy.36), calls=%async_computation.1 | async-start | bytes 917504 | tf_op jit(solution)/shard_map/all_to_all | solution.py:59
  29.5 456.1 %reduce-scatter.4.cloned.1.call-start = ((), (), s32[]{:S(2)}) async-start(), calls=%async_computation.4 | async-start | bytes 7798784
  53.9 10.1 %collective-permute-start = (bf16[16,2,7168]{2,1,0:T(2,128)(2,1)S(1)}, bf16[16,2,7168]{2,1,0:T(2,128)(2,1)S(1)}, u32[]{:S(2)}, u32[]{:S(2)}) collective-permute-start(bf16[16,2,7168]{2,1,0:T(2,128)(2,1)S(1)} %all-to-all-done.1), channel_id=1, source_target_pairs={{0,1},{1,2},{2,3},{3,4},{4,5},{5,6},{6,7},{7,8},{8,9},{9,10},{10,1... | collective-permute-start | bytes 1376264 | tf_op jit(solution)/shard_map/ppermute | solution.py:21
  55.3 11.3 %collective-permute-start.1 = (bf16[16,2,7168]{2,1,0:T(2,128)(2,1)S(1)}, bf16[16,2,7168]{2,1,0:T(2,128)(2,1)S(1)}, u32[]{:S(2)}, u32[]{:S(2)}) collective-permute-start(bf16[16,2,7168]{2,1,0:T(2,128)(2,1)S(1)} %all-to-all-done.1), channel_id=1, source_target_pairs={{0,15},{1,0},{2,1},{3,2},{4,3},{5,4},{6,5},{7,6},{8,7},{9,8},{10,9... | collective-permute-start | bytes 1376264 | tf_op jit(solution)/shard_map/ppermute | solution.py:28
  64.0 12.3 %collective-permute-start.2 = (bf16[16,2,7168]{2,1,0:T(2,128)(2,1)S(1)}, bf16[16,2,7168]{2,1,0:T(2,128)(2,1)S(1)}, u32[]{:S(2)}, u32[]{:S(2)}) collective-permute-start(bf16[16,2,7168]{2,1,0:T(2,128)(2,1)S(1)} %collective-permute-done), channel_id=1, source_target_pairs={{0,1},{1,2},{2,3},{3,4},{4,5},{5,6},{6,7},{7,8},{8,9},{9,10},{10,1... | collective-permute-start | bytes 1376264 | tf_op jit(solution)/shard_map/ppermute | solution.py:21
  66.6 12.2 %collective-permute-start.3 = (bf16[16,2,7168]{2,1,0:T(2,128)(2,1)S(1)}, bf16[16,2,7168]{2,1,0:T(2,128)(2,1)S(1)}, u32[]{:S(2)}, u32[]{:S(2)}) collective-permute-start(bf16[16,2,7168]{2,1,0:T(2,128)(2,1)S(1)} %collective-permute-done.1), channel_id=1, source_target_pairs={{0,15},{1,0},{2,1},{3,2},{4,3},{5,4},{6,5},{7,6},{8,7},{9,8},{10,9... | collective-permute-start | bytes 1376264 | tf_op jit(solution)/shard_map/ppermute | solution.py:28
  76.3 13.3 %collective-permute-start.4 = (bf16[16,2,7168]{2,1,0:T(2,128)(2,1)S(1)}, bf16[16,2,7168]{2,1,0:T(2,128)(2,1)S(1)}, u32[]{:S(2)}, u32[]{:S(2)}) collective-permute-start(bf16[16,2,7168]{2,1,0:T(2,128)(2,1)S(1)} %collective-permute-done.2), channel_id=1, source_target_pairs={{0,1},{1,2},{2,3},{3,4},{4,5},{5,6},{6,7},{7,8},{8,9},{9,10},{10,1... | collective-permute-start | bytes 1376264 | tf_op jit(solution)/shard_map/ppermute | solution.py:21
  78.7 13.3 %collective-permute-start.5 = (bf16[16,2,7168]{2,1,0:T(2,128)(2,1)S(1)}, bf16[16,2,7168]{2,1,0:T(2,128)(2,1)S(1)}, u32[]{:S(2)}, u32[]{:S(2)}) collective-permute-start(bf16[16,2,7168]{2,1,0:T(2,128)(2,1)S(1)} %collective-permute-done.3), channel_id=1, source_target_pairs={{0,15},{1,0},{2,1},{3,2},{4,3},{5,4},{6,5},{7,6},{8,7},{9,8},{10,9... | collective-permute-start | bytes 1376264 | tf_op jit(solution)/shard_map/ppermute | solution.py:28
  89.6 12.5 %collective-permute-start.6 = (bf16[16,2,7168]{2,1,0:T(2,128)(2,1)S(1)}, bf16[16,2,7168]{2,1,0:T(2,128)(2,1)S(1)}, u32[]{:S(2)}, u32[]{:S(2)}) collective-permute-start(bf16[16,2,7168]{2,1,0:T(2,128)(2,1)S(1)} %collective-permute-done.4), channel_id=1, source_target_pairs={{0,1},{1,2},{2,3},{3,4},{4,5},{5,6},{6,7},{7,8},{8,9},{9,10},{10,1... | collective-permute-start | bytes 1376264 | tf_op jit(solution)/shard_map/ppermute | solution.py:21
  92.1 12.5 %collective-permute-start.7 = (bf16[16,2,7168]{2,1,0:T(2,128)(2,1)S(1)}, bf16[16,2,7168]{2,1,0:T(2,128)(2,1)S(1)}, u32[]{:S(2)}, u32[]{:S(2)}) collective-permute-start(bf16[16,2,7168]{2,1,0:T(2,128)(2,1)S(1)} %collective-permute-done.5), channel_id=1, source_target_pairs={{0,15},{1,0},{2,1},{3,2},{4,3},{5,4},{6,5},{7,6},{8,7},{9,8},{10,9... | collective-permute-start | bytes 1376264 | tf_op jit(solution)/shard_map/ppermute | solution.py:28
  102.1 15.1 %collective-permute-start.8 = (bf16[16,2,7168]{2,1,0:T(2,128)(2,1)S(1)}, bf16[16,2,7168]{2,1,0:T(2,128)(2,1)S(1)}, u32[]{:S(2)}, u32[]{:S(2)}) collective-permute-start(bf16[16,2,7168]{2,1,0:T(2,128)(2,1)S(1)} %collective-permute-done.6), channel_id=1, source_target_pairs={{0,1},{1,2},{2,3},{3,4},{4,5},{5,6},{6,7},{7,8},{8,9},{9,10},{10,1... | collective-permute-start | bytes 1376264 | tf_op jit(solution)/shard_map/ppermute | solution.py:21
  104.6 12.7 %collective-permute-start.9 = (bf16[16,2,7168]{2,1,0:T(2,128)(2,1)S(1)}, bf16[16,2,7168]{2,1,0:T(2,128)(2,1)S(1)}, u32[]{:S(2)}, u32[]{:S(2)}) collective-permute-start(bf16[16,2,7168]{2,1,0:T(2,128)(2,1)S(1)} %collective-permute-done.7), channel_id=1, source_target_pairs={{0,15},{1,0},{2,1},{3,2},{4,3},{5,4},{6,5},{7,6},{8,7},{9,8},{10,9... | collective-permute-start | bytes 1376264 | tf_op jit(solution)/shard_map/ppermute | solution.py:28
  117.1 16.9 %collective-permute-start.10 = (bf16[16,2,7168]{2,1,0:T(2,128)(2,1)S(1)}, bf16[16,2,7168]{2,1,0:T(2,128)(2,1)S(1)}, u32[]{:S(2)}, u32[]{:S(2)}) collective-permute-start(bf16[16,2,7168]{2,1,0:T(2,128)(2,1)S(1)} %collective-permute-done.8), channel_id=1, source_target_pairs={{0,1},{1,2},{2,3},{3,4},{4,5},{5,6},{6,7},{7,8},{8,9},{9,10},{10,1... | collective-permute-start | bytes 1376264 | tf_op jit(solution)/shard_map/ppermute | solution.py:21
  117.3 16.8 %collective-permute-start.11 = (bf16[16,2,7168]{2,1,0:T(2,128)(2,1)S(1)}, bf16[16,2,7168]{2,1,0:T(2,128)(2,1)S(1)}, u32[]{:S(2)}, u32[]{:S(2)}) collective-permute-start(bf16[16,2,7168]{2,1,0:T(2,128)(2,1)S(1)} %collective-permute-done.9), channel_id=1, source_target_pairs={{0,15},{1,0},{2,1},{3,2},{4,3},{5,4},{6,5},{7,6},{8,7},{9,8},{10,9... | collective-permute-start | bytes 1376264 | tf_op jit(solution)/shard_map/ppermute | solution.py:28
  134.1 15.7 %collective-permute-start.12 = (bf16[16,2,7168]{2,1,0:T(2,128)(2,1)S(1)}, bf16[16,2,7168]{2,1,0:T(2,128)(2,1)S(1)}, u32[]{:S(2)}, u32[]{:S(2)}) collective-permute-start(bf16[16,2,7168]{2,1,0:T(2,128)(2,1)S(1)} %collective-permute-done.10), channel_id=1, source_target_pairs={{0,1},{1,2},{2,3},{3,4},{4,5},{5,6},{6,7},{7,8},{8,9},{9,10},{10,1... | collective-permute-start | bytes 1376264 | tf_op jit(solution)/shard_map/ppermute | solution.py:21
  134.1 16.8 %collective-permute-start.13 = (bf16[16,2,7168]{2,1,0:T(2,128)(2,1)S(1)}, bf16[16,2,7168]{2,1,0:T(2,128)(2,1)S(1)}, u32[]{:S(2)}, u32[]{:S(2)}) collective-permute-start(bf16[16,2,7168]{2,1,0:T(2,128)(2,1)S(1)} %collective-permute-done.11), channel_id=1, source_target_pairs={{0,15},{1,0},{2,1},{3,2},{4,3},{5,4},{6,5},{7,6},{8,7},{9,8},{10,9... | collective-permute-start | bytes 1376264 | tf_op jit(solution)/shard_map/ppermute | solution.py:28
  149.8 11.5 %collective-permute-start.14 = (bf16[16,2,7168]{2,1,0:T(2,128)(2,1)S(1)}, bf16[16,2,7168]{2,1,0:T(2,128)(2,1)S(1)}, u32[]{:S(2)}, u32[]{:S(2)}) collective-permute-start(bf16[16,2,7168]{2,1,0:T(2,128)(2,1)S(1)} %collective-permute-done.12), channel_id=1, source_target_pairs={{0,1},{1,2},{2,3},{3,4},{4,5},{5,6},{6,7},{7,8},{8,9},{9,10},{10,1... | collective-permute-start | bytes 1376264 | tf_op jit(solution)/shard_map/ppermute | solution.py:21
  391.5 95.9 %copy-start.1 = (bf16[4,7168]{1,0:T(4,128)(2,1)S(1)}, bf16[4,7168]{1,0:T(4,128)(2,1)}, u32[]{:S(2)}) copy-start(bf16[4,7168]{1,0:T(4,128)(2,1)} %param.7) | copy-start | bytes 172036
Sparse Core Ops, SparseCore 0:
  398.6 86.8 reduce-scatter.3
